TPU v7x, 512 devices: a whole 4x8x8 slice. The times are simulated.
512 devices in a mesh: gx: 4 (over x), gy: 16 (over z, core), gz: 8 (over y).
Axes of the slice: x: 4, y: 8, z: 8, core: 2. Of those that a mesh axis runs over, the one named last changes fastest.
Arguments:
- right_side: float32 [64, 128, 1024], P('gx', 'gy', 'gz'), may hold values from -24 to 24
- conduct: float32 [64, 128, 1024], P('gx', 'gy', 'gz'), may hold values from 0.3 to 3
- mass: float32 [64, 128, 1024], P('gx', 'gy', 'gz'), may hold values from 0.01 to 0.2
- aggregate_of: int32 [16, 32, 256], P('gx', 'gy', 'gz'), may hold values from 0 to 2047
- coarse_inverse: float32 [2048, 2048], P('gy'), as said below
Outputs:
- solution_field: float32 [64, 128, 1024], P('gx', 'gy', 'gz')
Inputs may be any that keep to these rules, and one draw needn't show every extreme that they name: coarse_inverse is symmetric.
All inputs are finite; a program needn't handle non-finite values.
Results may differ from a plain program's by a relative error of at most 0.00015.
Values sent between devices are 32-bit elements; how exact they have to be, the bound alone decides.
A program may use at most 64 MiB of HBM per device.

v0:
```python
import jax
import jax.numpy as jnp
from jax import lax
from jax.sharding import PartitionSpec as P

LEVELS = 3
CYCLES = 2


stencil_offsets = [
    (first, second, third)
    for first in (-1, 0, 1)
    for second in (-1, 0, 1)
    for third in (-1, 0, 1)
    if (first, second, third) != (0, 0, 0)
]
stencil_weights = (0.0, 1.0, 0.5, 0.25)
OMEGA = 0.7


def extended(value, sides, width):
    for axis, dim in sides:
        size, length = (lax.axis_size(axis), value.shape[dim])
        up = [(i, (i + 1) % size) for i in range(size - 1)]
        down = [(j, i) for i, j in up]
        last = lax.slice_in_dim(value, length - width, length, axis=dim)
        first = lax.slice_in_dim(value, 0, width, axis=dim)
        before = lax.ppermute(last, axis, up)
        after = lax.ppermute(first, axis, down)
        value = jnp.concatenate([before, value, after], axis=dim)
    return value


def shifted_sum(padded):
    shape = tuple((n - 2 for n in padded.shape))
    total = jnp.zeros(shape, jnp.float32)
    for offset in stencil_offsets:
        weight = stencil_weights[abs(offset[0]) + abs(offset[1]) + abs(offset[2])]
        piece = padded[
            1 + offset[0] : 1 + offset[0] + shape[0],
            1 + offset[1] : 1 + offset[1] + shape[1],
            1 + offset[2] : 1 + offset[2] + shape[2],
        ]
        total = total + weight * piece
    return total


def pool_sum(field):
    shape = field.shape
    return field.reshape(shape[0] // 2, 2, shape[1] // 2, 2, shape[2] // 2, 2).sum(axis=(1, 3, 5))


def spread_up(field):
    return jnp.repeat(jnp.repeat(jnp.repeat(field, 2, axis=0), 2, axis=1), 2, axis=2)


def conduct_halo(conduct_lv):
    return extended(conduct_lv - 1.0, (("gx", 0), ("gy", 1), ("gz", 2)), 1) + 1.0


def field_halo(field):
    return extended(field, (("gx", 0), ("gy", 1), ("gz", 2)), 1)


def apply_operator(field, level_data):
    padded_k, scaled_k, diagonal = level_data
    padded_v = field_halo(field)
    return diagonal * field - scaled_k * shifted_sum(padded_k * padded_v)


def sweep(field, source, level_data):
    diagonal = level_data[2]
    if field is None:
        return OMEGA * source / diagonal
    return field + OMEGA * (source - apply_operator(field, level_data)) / diagonal


def local(right_side, conduct, mass, aggregate_of, coarse_inverse):
    count = coarse_inverse.shape[1]
    data = []
    conduct_lv = conduct
    mass_lv = mass
    for level in range(LEVELS):
        padded_k = conduct_halo(conduct_lv)
        scaled_k = 2.0**level * conduct_lv
        diagonal = scaled_k * shifted_sum(padded_k) + mass_lv
        data.append((padded_k, scaled_k, diagonal))
        if level + 1 < LEVELS:
            conduct_lv = pool_sum(conduct_lv) * 0.125
            mass_lv = pool_sum(mass_lv)

    def aggregate_fix(residual):
        partial_sums = jax.ops.segment_sum(
            residual.reshape(-1), aggregate_of.reshape(-1), num_segments=count
        )
        totals = lax.psum(partial_sums, ("gx", "gy", "gz"))
        owned = jnp.dot(coarse_inverse, totals, precision=lax.Precision.HIGHEST)
        correction = lax.all_gather(owned, "gy", axis=0, tiled=True)
        return correction[aggregate_of]

    def cycle(level, source, field):
        field = sweep(field, source, data[level])
        field = sweep(field, source, data[level])
        residual = source - apply_operator(field, data[level])
        if level + 1 < LEVELS:
            field = field + spread_up(cycle(level + 1, pool_sum(residual), None))
        else:
            field = field + aggregate_fix(residual)
        field = sweep(field, source, data[level])
        field = sweep(field, source, data[level])
        return field

    solution = None
    for turn in range(CYCLES):
        solution = cycle(0, right_side, solution)
    return solution


def solution(mesh):
    return jax.shard_map(
        local,
        mesh=mesh,
        in_specs=(
            P("gx", "gy", "gz"),
            P("gx", "gy", "gz"),
            P("gx", "gy", "gz"),
            P("gx", "gy", "gz"),
            P("gy", None),
        ),
        out_specs=P("gx", "gy", "gz"),
        check_vma=False,
    )
```

profile of v0, /device:TPU:1, one launch (start us, length us, event | category | flops | bytes accessed | tf_op | source)
XLA Modules:
  0.0 975.5 jit_solution(8087658498856792512)
XLA Ops:
  6.2 6.3 reshape.68
  53.6 5.5 reshape.69
  86.6 5.2 collective-permute-start.14
  108.6 5.4 collective-permute-done.17
  114.7 5.5 reshape.67
  130.5 5.5 collective-permute-start.26
  160.1 5.4 collective-permute-start.32
  174.1 5.6 collective-permute-start.34
  191.7 7.1 collective-permute-start.44
  240.9 103.9 %psum.14 = f32[2048]{0:T(1024)S(1)} all-reduce(f32[2048]{0:T(1024)S(1)} %scatter_custom_fusion), channel_id=1, replica_groups=mesh['gx'=4,'gy'=16,'gz'=8] {'gx','gy','gz'}, use_global_device_ids=true, to_apply=%region_7.0 | all-reduce | flops 2048 | bytes 16384 | tf_op jit(solution)/shard_map/psum | solution.py:96
  345.7 15.9 %all-gather = f32[16,1,128]{2,1,0:T(1,128)S(1)} all-gather(f32[1,1,128]{2,1,0:T(1,128)S(1)} %convolution_bitcast_fusion.1), channel_id=1, replica_groups=mesh['gx'=4,'gy'=16,'gz'=8] {'gy'}, dimensions={0}, use_global_device_ids=true | all-gather | bytes 8704 | tf_op jit(solution)/shard_map/all_gather | solution.py:98
  469.6 5.2 collective-permute-start.80
  494.8 5.3 collective-permute-start.86
  520.6 6.0 collective-permute-start.92
  547.0 5.8 collective-permute-start.98
  573.5 5.8 collective-permute-start.104
  593.7 5.5 reshape.79
  607.8 5.8 collective-permute-start.110
  632.7 5.9 collective-permute-start.116
  658.3 5.9 collective-permute-start.122
  682.7 6.1 collective-permute-start.128
  703.4 101.3 %psum.15 = f32[2048]{0:T(1024)S(1)} all-reduce(f32[2048]{0:T(1024)S(1)} %scatter_custom_fusion.1), channel_id=1, replica_groups=mesh['gx'=4,'gy'=16,'gz'=8] {'gx','gy','gz'}, use_global_device_ids=true, to_apply=%region_11.0 | all-reduce | flops 2048 | bytes 16384 | tf_op jit(solution)/shard_map/psum | solution.py:96
  805.6 16.3 %all-gather.1 = f32[16,1,128]{2,1,0:T(1,128)S(1)} all-gather(f32[1,1,128]{2,1,0:T(1,128)S(1)} %convolution_bitcast_fusion), channel_id=1, replica_groups=mesh['gx'=4,'gy'=16,'gz'=8] {'gy'}, dimensions={0}, use_global_device_ids=true | all-gather | bytes 8704 | tf_op jit(solution)/shard_map/all_gather | solution.py:98
  954.9 5.3 collective-permute-start.164
  (612 shorter events, 620.1 us)
Async XLA Ops:
  0.9 14.1 %collective-permute-start = (f32[1,8,128]{2,1,0:T(8,128)S(1)}, f32[1,8,128]{2,1,0:T(8,128)S(1)}, u32[]{:S(2)}, u32[]{:S(2)}) collective-permute-start(f32[1,8,128]{2,1,0:T(8,128)S(1)} %get-tuple-element.69), channel_id=1, source_target_pairs={{0,128},{128,256},{256,384},{1,129},{129,257},{257,385},{2,130},{1... | collective-permute-start | bytes 12296 | tf_op jit(solution)/shard_map/ppermute | solution.py:28
  4.9 10.2 %collective-permute-start.1 = (f32[1,8,128]{2,1,0:T(8,128)S(1)}, f32[1,8,128]{2,1,0:T(8,128)S(1)}, u32[]{:S(2)}, u32[]{:S(2)}) collective-permute-start(f32[1,8,128]{2,1,0:T(8,128)S(1)} %get-tuple-element.70), channel_id=1, source_target_pairs={{128,0},{256,128},{384,256},{129,1},{257,129},{385,257},{130,2},{2... | collective-permute-start | bytes 12296 | tf_op jit(solution)/shard_map/ppermute | solution.py:29
  25.1 10.8 %collective-permute-start.4 = (f32[18,10,1]{2,0,1:T(8,128)S(1)}, f32[18,10,1]{2,0,1:T(8,128)S(1)}, u32[]{:S(2)}, u32[]{:S(2)}) collective-permute-start(f32[18,10,1]{2,0,1:T(8,128)S(1)} %get-tuple-element.29), channel_id=1, source_target_pairs={{0,1},{1,2},{2,3},{3,4},{4,5},{5,6},{6,7},{8,9},{9,10},{10,11},{11... | collective-permute-start | bytes 2168 | tf_op jit(solution)/shard_map/ppermute | solution.py:28
  29.6 42.2 %collective-permute-start.18 = (f32[1,4,64]{2,1,0:T(4,128)S(1)}, f32[1,4,64]{2,1,0:T(4,128)S(1)}, u32[]{:S(2)}, u32[]{:S(2)}) collective-permute-start(f32[1,4,64]{2,1,0:T(4,128)S(1)} %get-tuple-element.143), channel_id=1, source_target_pairs={{0,128},{128,256},{256,384},{1,129},{129,257},{257,385},{2,130},{1... | collective-permute-start | bytes 3080 | tf_op jit(solution)/shard_map/ppermute | solution.py:28
  33.9 39.2 %collective-permute-start.19 = (f32[1,4,64]{2,1,0:T(4,128)S(1)}, f32[1,4,64]{2,1,0:T(4,128)S(1)}, u32[]{:S(2)}, u32[]{:S(2)}) collective-permute-start(f32[1,4,64]{2,1,0:T(4,128)S(1)} %get-tuple-element.144), channel_id=1, source_target_pairs={{128,0},{256,128},{384,256},{129,1},{257,129},{385,257},{130,2},{2... | collective-permute-start | bytes 3080 | tf_op jit(solution)/shard_map/ppermute | solution.py:29
  44.9 17.5 %collective-permute-start.8 = (f32[18,1,128]{2,1,0:T(1,128)S(1)}, f32[18,1,128]{2,1,0:T(1,128)S(1)}, u32[]{:S(2)}, u32[]{:S(2)}) collective-permute-start(f32[18,1,128]{2,1,0:T(1,128)S(1)} %get-tuple-element.48), channel_id=1, source_target_pairs={{0,8},{8,16},{16,24},{24,32},{32,40},{40,48},{48,56},{56,64},{64,7... | collective-permute-start | bytes 27656 | tf_op jit(solution)/shard_map/ppermute | solution.py:28
  49.2 78.0 %collective-permute-start.36 = (f32[1,2,32]{2,0,1:T(1,128)S(1)}, f32[1,2,32]{2,0,1:T(1,128)S(1)}, u32[]{:S(2)}, u32[]{:S(2)}) collective-permute-start(f32[1,2,32]{2,0,1:T(1,128)S(1)} %get-tuple-element.179), channel_id=1, source_target_pairs={{0,128},{128,256},{256,384},{1,129},{129,257},{257,385},{2,130},{1... | collective-permute-start | bytes 776 | tf_op jit(solution)/shard_map/ppermute | solution.py:28
  52.3 74.9 %collective-permute-start.37 = (f32[1,2,32]{2,0,1:T(1,128)S(1)}, f32[1,2,32]{2,0,1:T(1,128)S(1)}, u32[]{:S(2)}, u32[]{:S(2)}) collective-permute-start(f32[1,2,32]{2,0,1:T(1,128)S(1)} %get-tuple-element.180), channel_id=1, source_target_pairs={{128,0},{256,128},{384,256},{129,1},{257,129},{385,257},{130,2},{2... | collective-permute-start | bytes 776 | tf_op jit(solution)/shard_map/ppermute | solution.py:29
  67.5 7.9 collective-permute-start.10
  73.1 9.1 collective-permute-start.20
  75.4 8.2 collective-permute-start.21
  86.6 10.6 %collective-permute-start.14 = (f32[18,1,128]{2,1,0:T(1,128)S(1)}, f32[18,1,128]{2,1,0:T(1,128)S(1)}, u32[]{:S(2)}, u32[]{:S(2)}) collective-permute-start(f32[18,1,128]{2,1,0:T(1,128)S(1)} %get-tuple-element.46), channel_id=1, source_target_pairs={{0,8},{8,16},{16,24},{24,32},{32,40},{40,48},{48,56},{56,64},{64,7... | collective-permute-start | bytes 27656 | tf_op jit(solution)/shard_map/ppermute | solution.py:28
  91.9 14.9 %collective-permute-start.22 = (f32[10,6,1]{2,1,0:T(8,128)S(1)}, f32[10,6,1]{2,1,0:T(8,128)S(1)}, u32[]{:S(2)}, u32[]{:S(2)}) collective-permute-start(f32[10,6,1]{2,1,0:T(8,128)S(1)} %get-tuple-element.87), channel_id=1, source_target_pairs={{0,1},{1,2},{2,3},{3,4},{4,5},{5,6},{6,7},{8,9},{9,10},{10,11},{11... | collective-permute-start | bytes 728 | tf_op jit(solution)/shard_map/ppermute | solution.py:28
  95.9 12.2 %collective-permute-start.23 = (f32[10,6,1]{2,1,0:T(8,128)S(1)}, f32[10,6,1]{2,1,0:T(8,128)S(1)}, u32[]{:S(2)}, u32[]{:S(2)}) collective-permute-start(f32[10,6,1]{2,1,0:T(8,128)S(1)} %get-tuple-element.88), channel_id=1, source_target_pairs={{1,0},{2,1},{3,2},{4,3},{5,4},{6,5},{7,6},{9,8},{10,9},{11,10},{12... | collective-permute-start | bytes 728 | tf_op jit(solution)/shard_map/ppermute | solution.py:29
  141.1 12.3 %collective-permute-start.28 = (f32[10,6,1]{2,1,0:T(8,128)S(1)}, f32[10,6,1]{2,1,0:T(8,128)S(1)}, u32[]{:S(2)}, u32[]{:S(2)}) collective-permute-start(f32[10,6,1]{2,1,0:T(8,128)S(1)} %get-tuple-element.85), channel_id=1, source_target_pairs={{0,1},{1,2},{2,3},{3,4},{4,5},{5,6},{6,7},{8,9},{9,10},{10,11},{11... | collective-permute-start | bytes 728 | tf_op jit(solution)/shard_map/ppermute | solution.py:28
  145.5 7.9 collective-permute-start.29
  146.8 10.3 %collective-permute-start.38 = (f32[6,1,32]{2,0,1:T(8,128)S(1)}, f32[6,1,32]{2,0,1:T(8,128)S(1)}, u32[]{:S(2)}, u32[]{:S(2)}) collective-permute-start(f32[6,1,32]{2,0,1:T(8,128)S(1)} %get-tuple-element.161), channel_id=1, source_target_pairs={{0,8},{8,16},{16,24},{24,32},{32,40},{40,48},{48,56},{56,64},{64,7... | collective-permute-start | bytes 2312 | tf_op jit(solution)/shard_map/ppermute | solution.py:28
  160.1 13.9 %collective-permute-start.32 = (f32[10,1,64]{2,1,0:T(1,128)S(1)}, f32[10,1,64]{2,1,0:T(1,128)S(1)}, u32[]{:S(2)}, u32[]{:S(2)}) collective-permute-start(f32[10,1,64]{2,1,0:T(1,128)S(1)} %get-tuple-element.101), channel_id=1, source_target_pairs={{0,8},{8,16},{16,24},{24,32},{32,40},{40,48},{48,56},{56,64},{64,7... | collective-permute-start | bytes 7688 | tf_op jit(solution)/shard_map/ppermute | solution.py:28
  165.5 8.5 collective-permute-start.33
  167.5 14.0 %collective-permute-start.40 = (f32[6,4,1]{2,0,1:T(8,128)S(1)}, f32[6,4,1]{2,0,1:T(8,128)S(1)}, u32[]{:S(2)}, u32[]{:S(2)}) collective-permute-start(f32[6,4,1]{2,0,1:T(8,128)S(1)} %get-tuple-element.135), channel_id=1, source_target_pairs={{0,1},{1,2},{2,3},{3,4},{4,5},{5,6},{6,7},{8,9},{9,10},{10,11},{11... | collective-permute-start | bytes 296 | tf_op jit(solution)/shard_map/ppermute | solution.py:28
  172.7 8.8 collective-permute-start.41
  191.7 9.0 collective-permute-start.44
  520.6 7.9 collective-permute-start.92
  682.7 8.0 collective-permute-start.128
  (149 other events, 1221.5 us)
where the time goes:
time: 992 us; the launch traced here: 975 us
  starting transfers between devices  433 us (44%)
  waiting for transfers between devices  238 us (24%)
  blocking collectives  237 us (24%)
  local copies, waits for them, and re-layouts  33 us (3%)
  other arithmetic  28.4 us (3%)
    ppermute x84, starting transfers between devices, extended(): before = lax.ppermute(last, axis, up)  305 us
    ppermute x84, waiting for transfers between devices, extended(): after = lax.ppermute(first, axis, down)  234 us
    psum x2, blocking collectives, aggregate_fix(): totals = lax.psum(partial_sums, ('gx', 'gy', 'gz'))  205 us
    ppermute x84, starting transfers between devices, extended(): after = lax.ppermute(first, axis, down)  128 us
    all_gather x2, blocking collectives, aggregate_fix(): correction = lax.all_gather(owned, 'gy', axis=0, tiled=True)  32.2 us
    reshape x7, local copies, waits for them, and re-layouts, pool_sum(): field.reshape(shape[0] // 2, 2, shape[1] // 2, 2, shape[2] // 2, 2)  24.5 us
  transfers between devices with their start and end apart: 168, of which 82 were waited for; matrix products, arithmetic and copies ran while one was open for 3% of the time, Pallas kernels for 0%

commit v1 on v0

v1 whole, which is shorter than its diff:
```python
import jax
import jax.numpy as jnp
from jax import lax
from jax.experimental import pallas as pl
from jax.experimental.pallas import tpu as pltpu
from jax.sharding import PartitionSpec as P

CYCLES = 2
OMEGA = 0.7
F32 = jnp.float32
BF16 = jnp.bfloat16
MESH = pl.DeviceIdType.MESH

SIZE = ((16, 8, 128), (8, 4, 64), (4, 2, 32))
PLANES = (24, 16, 12)
LANES = (256, 128, 128)
REACH = (1, 1, 2)
ROWS = 16
HALO = 4
AXES = ("gx", "gy", "gz")
COUNT = {"gx": 4, "gy": 16, "gz": 8}

EXCHANGES = [(0, 3), (1, 2), (2, 2)]
for turn in range(CYCLES):
    EXCHANGES += [(1, 1), (2, 1), (2, 1), (1, 1)]
    if turn + 1 < CYCLES:
        EXCHANGES += [(0, 1)]


def exchange_scratch(level, fields):
    nx = SIZE[level][0]
    planes = PLANES[level]
    reach = REACH[level]
    copies = 4 + 2 * reach
    return [
        pltpu.VMEM((fields, nx, 8, 128), F32),
        pltpu.VMEM((2, fields, HALO, 8, 128), F32),
        pltpu.VMEM((fields, planes, 8, 128), F32),
        pltpu.VMEM((2 * reach, fields, planes, 8, 128), F32),
        pltpu.VMEM((2, fields, ROWS, 128), F32),
        pltpu.VMEM((2, fields, ROWS, 128), F32),
        pltpu.SemaphoreType.DMA((copies,)),
        pltpu.SemaphoreType.DMA((copies,)),
    ]


def coarse_scratch():
    return [
        pltpu.VMEM((16, 1, 128), F32),
        pltpu.VMEM((16, 1, 128), F32),
        pltpu.VMEM((1, 128), F32),
        pltpu.VMEM((4, 1, 128), F32),
        pltpu.VMEM((1, 128), F32),
        pltpu.VMEM((8, 1, 128), F32),
        pltpu.VMEM((16, 128), F32),
        pltpu.VMEM((16, 16, 128), F32),
        pltpu.SemaphoreType.DMA((41,)),
        pltpu.SemaphoreType.DMA((41,)),
    ]


PER_EXCHANGE = 8
PER_COARSE = 10


def peer(axis, step):
    return lax.rem(lax.axis_index(axis) + (step + COUNT[axis]), COUNT[axis])


def send(src, dst, send_sem, recv_sem, axis, step):
    copy = pltpu.make_async_remote_copy(
        src_ref=src,
        dst_ref=dst,
        send_sem=send_sem,
        recv_sem=recv_sem,
        device_id={axis: peer(axis, step)},
        device_id_type=MESH,
    )
    copy.start()
    return copy


def iota(shape, dim):
    return lax.broadcasted_iota(jnp.int32, shape, dim)


def turn_by(value, shift, axis):
    size = value.shape[axis]
    shift = shift % size
    if shift == 0:
        return value
    return pltpu.roll(value, shift, axis)


def exchange(jobs):
    copies = []
    for level, bufs, fields in jobs:
        own, from_x, _, _, _, _, ss, rs = bufs
        nx = SIZE[level][0]
        for i, value in enumerate(fields):
            own[i] = value
        copies.append(send(own.at[:, 0:HALO], from_x.at[0], ss.at[0], rs.at[0], "gx", -1))
        copies.append(send(own.at[:, nx - HALO : nx], from_x.at[1], ss.at[1], rs.at[1], "gx", 1))
    for copy in copies:
        copy.wait()
    copies = []
    for level, bufs, fields in jobs:
        own, from_x, slab, from_y, _, _, ss, rs = bufs
        nx = SIZE[level][0]
        for i in range(len(fields)):
            slab[i, 0:nx] = own[i]
            slab[i, nx : nx + HALO] = from_x[0, i]
            slab[i, nx + HALO : nx + 2 * HALO] = from_x[1, i]
        for step in range(1, REACH[level] + 1):
            for side, way in ((0, -1), (1, 1)):
                at = 2 * (step - 1) + side
                copies.append(send(slab, from_y.at[at], ss.at[2 + at], rs.at[2 + at], "gy", way * step))
    for copy in copies:
        copy.wait()
    copies = []
    columns = []
    for level, bufs, fields in jobs:
        _, _, slab, from_y, edges, from_z, ss, rs = bufs
        planes = PLANES[level]
        nz = SIZE[level][2]
        row = iota((planes, 8, 128), 1)
        lane = iota((ROWS, 128), 1)
        mine = []
        for i in range(len(fields)):
            value = slab[i]
            if level == 0:
                first = value
                second = jnp.where(row < 4, from_y[0, i], from_y[1, i])
            elif level == 1:
                first = jnp.where(row < 4, value, turn_by(from_y[0, i], 4, 1))
                second = turn_by(from_y[1, i], 4, 1)
            else:
                far = jnp.where(row < 4, turn_by(from_y[0, i], 2, 1), turn_by(from_y[2, i], 4, 1))
                first = jnp.where(row < 2, value, far)
                second = jnp.where(row < 6, turn_by(from_y[3, i], 4, 1), turn_by(from_y[1, i], 6, 1))
            column = jnp.concatenate([first, second], axis=1)
            mine.append(column)
            low = jnp.zeros((ROWS, 128), F32)
            high = jnp.zeros((ROWS, 128), F32)
            for p in range(planes):
                here = (lane >= 4 * p) & (lane < 4 * p + 4)
                low = jnp.where(here, turn_by(column[p], 4 * p, 1), low)
                high = jnp.where(here, turn_by(column[p], 4 * p - (nz - 4), 1), high)
            edges[0, i] = low
            edges[1, i] = high
        columns.append(mine)
        at = 2 + 2 * REACH[level]
        copies.append(send(edges.at[0], from_z.at[0], ss.at[at], rs.at[at], "gz", -1))
        copies.append(send(edges.at[1], from_z.at[1], ss.at[at + 1], rs.at[at + 1], "gz", 1))
    for copy in copies:
        copy.wait()
    rings = []
    for (level, bufs, fields), mine in zip(jobs, columns):
        from_z = bufs[5]
        planes = PLANES[level]
        nz = SIZE[level][2]
        lane = iota((ROWS, 128), 1)
        out = []
        for i in range(len(fields)):
            right = from_z[0, i]
            left = from_z[1, i]
            made = []
            for p in range(planes):
                after = turn_by(right, nz - 4 * p, 1)
                before = turn_by(left, 124 - 4 * p, 1)
                if level == 0:
                    side = jnp.where(lane < 64, after, before)
                    made.append(jnp.concatenate([mine[i][p], side], axis=1))
                else:
                    side = jnp.where(lane < 100, after, before)
                    made.append(jnp.where(lane < nz, mine[i][p], side))
            out.append(jnp.stack(made, axis=0))
        rings.append(out)
    return rings


def ring_offset(index, own, length):
    return jnp.where(index < own + HALO, index, index - length)


def inside(level):
    shape = (PLANES[level], ROWS, LANES[level])
    result = None
    for dim, axis in enumerate(AXES):
        own = SIZE[level][dim]
        off = ring_offset(iota(shape, dim), own, shape[dim])
        place = off + lax.axis_index(axis) * own
        good = (place >= 0) & (place < COUNT[axis] * own) & (off >= -HALO)
        result = good if result is None else result & good
    return result


def smooth_sum(value):
    total = 2.0 * value
    total = total + jnp.concatenate([value[1:], value[:1]], axis=0)
    total = total + jnp.concatenate([value[-1:], value[:-1]], axis=0)
    total = 2.0 * total + turn_by(total, 1, 1) + turn_by(total, -1, 1)
    total = 2.0 * total + turn_by(total, 1, 2) + turn_by(total, -1, 2)
    return 0.25 * total - 2.0 * value


def parts(value):
    high = value.astype(BF16)
    rest = value - high.astype(F32)
    mid = rest.astype(BF16)
    low = (rest - mid.astype(F32)).astype(BF16)
    return high, mid, low


def times_right(value, chosen):
    return sum(jnp.dot(piece, chosen, preferred_element_type=F32) for piece in parts(value))


def times_left(chosen, value):
    return sum(jnp.dot(chosen, piece, preferred_element_type=F32) for piece in parts(value))


def as_chosen(condition):
    return jnp.where(condition, 1.0, 0.0).astype(BF16)


def pool_matrices(level):
    nx, ny, nz = SIZE[level]
    shape = (nx * 4, nx * 8)
    i, j = iota(shape, 0), iota(shape, 1)
    x_match = (i >> 3) == (j >> 4)
    y_match = (i & 7) == ((j & 7) >> 1)
    rows = as_chosen(x_match & y_match & ((j & 7) < ny))
    i, j = iota((128, 128), 0), iota((128, 128), 1)
    lanes = as_chosen(((i >> 1) == j) & (i < nz))
    return rows, lanes


def pool(value, matrices):
    planes = value.shape[0]
    flat = value.reshape(planes * 8, 128)
    small = times_left(matrices[0], times_right(flat, matrices[1]))
    return small.reshape(planes // 2, 8, 128)


def coarse_index(index, level, dim, length, coarse_length):
    off = ring_offset(index, SIZE[level][dim], length) >> 1
    return jnp.where(off < 0, off + coarse_length, off)


def spread_matrices(level):
    shape = (PLANES[level] * ROWS, PLANES[level + 1] * ROWS)
    i, j = iota(shape, 0), iota(shape, 1)
    x_match = coarse_index(i >> 4, level, 0, PLANES[level], PLANES[level + 1]) == (j >> 4)
    y_match = coarse_index(i & 15, level, 1, ROWS, ROWS) == (j & 15)
    rows = as_chosen(x_match & y_match)
    shape = (128, LANES[level])
    i, j = iota(shape, 0), iota(shape, 1)
    lanes = as_chosen(coarse_index(j, level, 2, LANES[level], 128) == i)
    return rows, lanes


def spread(value, matrices, level):
    flat = value.reshape(PLANES[level + 1] * ROWS, 128)
    wide = times_left(matrices[0], times_right(flat, matrices[1]))
    return wide.reshape(PLANES[level], ROWS, LANES[level])


def kernel(f_ref, k_ref, m_ref, agg_ref, inverse_ref, out_ref, *scratch):
    n_ex = len(EXCHANGES) * PER_EXCHANGE
    ex_bufs = [scratch[PER_EXCHANGE * e : PER_EXCHANGE * (e + 1)] for e in range(len(EXCHANGES))]
    co_bufs = [scratch[n_ex + PER_COARSE * c : n_ex + PER_COARSE * (c + 1)] for c in range(CYCLES)]
    keep = scratch[n_ex + PER_COARSE * CYCLES :]
    coef = keep[0:15]
    onehot_lo, onehot_hi, state0, state1 = keep[15:19]
    source = keep[19:22]

    barrier = pltpu.get_barrier_semaphore()
    for axis in AXES:
        for step in range(1, COUNT[axis]):
            pl.semaphore_signal(barrier, inc=1, device_id={axis: peer(axis, step)}, device_id_type=MESH)
    pl.semaphore_wait(barrier, sum(COUNT[axis] - 1 for axis in AXES))

    pools = [pool_matrices(0), pool_matrices(1)]
    ks, ms = [k_ref[...]], [m_ref[...]]
    for level in range(2):
        ks.append(pool(ks[level], pools[level]) * 0.125)
        ms.append(pool(ms[level], pools[level]))
    used = iter(ex_bufs)
    rings = exchange(
        [
            (0, next(used), [ks[0], ms[0], f_ref[...]]),
            (1, next(used), [ks[1], ms[1]]),
            (2, next(used), [ks[2], ms[2]]),
        ]
    )
    for level in range(3):
        kp_ref, sk_ref, d_ref, g_ref, in_ref = coef[5 * level : 5 * level + 5]
        ok = inside(level)
        kp = jnp.where(ok, rings[level][0], 1.0)
        scaled = 2.0**level * kp
        diagonal = scaled * smooth_sum(kp) + rings[level][1]
        kp_ref[...] = kp
        sk_ref[...] = scaled
        d_ref[...] = diagonal
        g_ref[...] = jnp.where(ok, OMEGA / diagonal, 0.0)
        in_ref[...] = jnp.where(ok, 1.0, 0.0)
    source[0][...] = rings[0][2]

    lanes_of = iota((128, 128), 0)
    highs = iota((16, 128), 0)
    for i in range(8):
        row = agg_ref[i : i + 1, :]
        onehot_lo[:, 128 * i : 128 * i + 128] = as_chosen(((row & 127) == lanes_of) & (row >= 0))
        onehot_hi[:, 128 * i : 128 * i + 128] = jnp.where((row >> 7) == highs, 1.0, 0.0)

    def residual(level, value):
        kp_ref, sk_ref, d_ref, _, _ = coef[5 * level : 5 * level + 5]
        around = smooth_sum(kp_ref[...] * value)
        return source[level][...] - d_ref[...] * value + sk_ref[...] * around

    def sweep(level, value):
        return value + coef[5 * level + 3][...] * residual(level, value)

    def start(level):
        return coef[5 * level + 3][...] * source[level][...]

    def swap(level, block):
        return exchange([(level, next(used), [block])])[0][0]

    def aggregate_fix(rest, bufs):
        mine, from_gy, at_gy, from_gx, at_gx, from_gz, partial, pieces, ss, rs = bufs
        rows = [rest[i // 2, i % 2 : i % 2 + 1, :] for i in range(8)]
        left = jnp.concatenate([onehot_hi[:, 128 * i : 128 * i + 128] * rows[i] for i in range(8)], axis=1)
        sums = sum(
            lax.dot_general(piece, onehot_lo[...], (((1,), (1,)), ((), ())), preferred_element_type=F32)
            for piece in parts(left)
        )
        for j in range(16):
            mine[j] = sums[j : j + 1, :]
        copies = []
        for step in range(1, 16):
            copies.append(send(mine.at[peer("gy", step)], from_gy.at[step], ss.at[step], rs.at[step], "gy", step))
        for copy in copies:
            copy.wait()
        total = mine[lax.axis_index("gy")]
        for step in range(1, 16):
            total = total + from_gy[step]
        at_gy[...] = total
        copies = []
        for step in range(1, 4):
            copies.append(send(at_gy, from_gx.at[step], ss.at[15 + step], rs.at[15 + step], "gx", step))
        for copy in copies:
            copy.wait()
        for step in range(1, 4):
            total = total + from_gx[step]
        at_gx[...] = total
        copies = []
        for step in range(1, 8):
            copies.append(send(at_gx, from_gz.at[step], ss.at[18 + step], rs.at[18 + step], "gz", step))
        for copy in copies:
            copy.wait()
        for step in range(1, 8):
            total = total + from_gz[step]
        down = jnp.broadcast_to(total, (128, 128)).T
        for j in range(16):
            product = down * inverse_ref[:, 128 * j : 128 * j + 128]
            partial[j : j + 1, :] = jnp.sum(product, axis=0, keepdims=True)
        copies = []
        for step in range(1, 16):
            at = 25 + step
            copies.append(send(partial, pieces.at[step], ss.at[at], rs.at[at], "gy", step))
        for copy in copies:
            copy.wait()
        fixes = partial[...]
        for step in range(1, 16):
            fixes = fixes + pieces[step]
        wide = times_right(fixes, onehot_lo[...])
        cells = jnp.sum(wide * onehot_hi[...], axis=0, keepdims=True)
        row = iota((8, 128), 0)
        planes = []
        for x in range(4):
            even = cells[:, 256 * x : 256 * x + 128]
            odd = cells[:, 256 * x + 128 : 256 * x + 256]
            planes.append(jnp.where(row == 0, even, jnp.where(row == 1, odd, 0.0)))
        return jnp.stack(planes, axis=0)

    value = start(0)
    for turn in range(CYCLES):
        if turn > 0:
            value = sweep(0, value)
        value = sweep(0, value)
        rest = residual(0, value)[0:16, 0:8, 0:128]
        state0[...] = value
        source[1][...] = swap(1, pool(rest, pools[0]))
        value = sweep(1, start(1))
        rest = residual(1, value)[0:8, 0:8, :]
        state1[...] = value
        source[2][...] = swap(2, pool(rest, pools[1]))
        value = sweep(2, start(2))
        rest = residual(2, value)[0:4, 0:8, :]
        fixed = value[0:4, 0:8, :] + aggregate_fix(rest, co_bufs[turn])
        value = swap(2, fixed) * coef[14][...]
        value = sweep(2, sweep(2, value))
        value = state1[...] + spread(value, spread_matrices(1), 1)
        value = sweep(1, sweep(1, value))
        value = swap(1, value[0:8, 0:8, :]) * coef[9][...]
        value = state0[...] + spread(value, spread_matrices(0), 0)
        value = sweep(0, sweep(0, value))
        if turn + 1 < CYCLES:
            value = swap(0, value[0:16, 0:8, 0:128]) * coef[4][...]
    out_ref[...] = value[0:16, 0:8, 0:128]


def local(right_side, conduct, mass, aggregate_of, coarse_inverse):
    agg = jnp.pad(aggregate_of.reshape(8, 32), ((0, 0), (0, 96)), constant_values=-1)
    scratch = []
    for level, fields in EXCHANGES:
        scratch += exchange_scratch(level, fields)
    for _ in range(CYCLES):
        scratch += coarse_scratch()
    rings = [pltpu.VMEM((PLANES[level], ROWS, LANES[level]), F32) for level in range(3)]
    for ring in rings:
        scratch += [ring] * 5
    scratch += [pltpu.VMEM((128, 1024), BF16), pltpu.VMEM((16, 1024), F32), rings[0], rings[1]]
    scratch += rings
    return pl.pallas_call(
        kernel,
        out_shape=jax.ShapeDtypeStruct(right_side.shape, F32),
        in_specs=[pl.BlockSpec(memory_space=pltpu.VMEM)] * 5,
        out_specs=pl.BlockSpec(memory_space=pltpu.VMEM),
        scratch_shapes=scratch,
        compiler_params=pltpu.CompilerParams(collective_id=0, has_side_effects=True),
    )(right_side, conduct, mass, agg, coarse_inverse)


def solution(mesh):
    return jax.shard_map(
        local,
        mesh=mesh,
        in_specs=(
            P("gx", "gy", "gz"),
            P("gx", "gy", "gz"),
            P("gx", "gy", "gz"),
            P("gx", "gy", "gz"),
            P("gy", None),
        ),
        out_specs=P("gx", "gy", "gz"),
        check_vma=False,
    )
```

time: 992 us -> 174 us (0.18); the launches traced: 975 us -> 174 us
  starting transfers between devices: 433 us -> 0 us
  waiting for transfers between devices: 238 us -> 0 us
  blocking collectives: 237 us -> 0 us
  Pallas kernels: 0 us -> 171 us
  local copies, waits for them, and re-layouts: 33 us -> 2.76 us
  other arithmetic: 28.4 us -> 0 us
    ppermute x168 -> x0, starting transfers between devices: 433 us -> none  [the longest x84 305 us: extended(): before = lax.ppermute(last, axis, up)]
    ppermute x168 -> x0, waiting for transfers between devices: 238 us -> none  [the longest x84 234 us: extended(): after = lax.ppermute(first, axis, down)]
    psum x2 -> x0, blocking collectives: 205 us -> none  [aggregate_fix(): totals = lax.psum(partial_sums, ('gx', 'gy', 'gz'))]
    pallas_call x0 -> x1, Pallas kernels: none -> 171 us  [local(): pl.pallas_call(kernel, out_shape=jax.ShapeDtypeStruct(right_side.shape, F...]
    all_gather x2 -> x0, blocking collectives: 32.2 us -> none  [aggregate_fix(): correction = lax.all_gather(owned, 'gy', axis=0, tiled=True)]
    reshape x17 -> x0, local copies, waits for them, and re-layouts: 25.6 us -> none  [the longest x7 24.5 us: pool_sum(): field.reshape(shape[0] // 2, 2, shape[1] // 2, 2, shape[2] // 2, 2)]
    reduce_sum x8 -> x0, other arithmetic: 10.7 us -> none  [pool_sum(): field.reshape(shape[0] // 2, 2, shape[1] // 2, 2, shape[2] // 2, 2)]
  transfers between devices with their start and end apart: 168 -> 0, of which waited for: 82 -> 0; matrix products, arithmetic and copies ran while one was open for 3% -> 0% of each run, Pallas kernels for 0% -> 0%
where the time goes in v1:
time: 174 us
  Pallas kernels  171 us (98%)
  local copies, waits for them, and re-layouts  2.76 us (2%)
    pallas_call x1, Pallas kernels, local(): pl.pallas_call(kernel, out_shape=jax.ShapeDtypeStruct(right_side.shape, F...  171 us

profile of v1, /device:TPU:1, one launch (start us, length us, event | category | flops | bytes accessed | tf_op | source)
XLA Modules:
  0.0 174.2 jit_solution(8104258559819602148)
XLA Ops:
  0.0 1.3 pad.4.agg_ref
  1.3 171.5 %shard_map.55 = f32[16,8,128]{2,1,0:T(8,128)} custom-call(f32[16,8,128]{2,1,0:T(8,128)} %f_ref.1, f32[16,8,128]{2,1,0:T(8,128)} %k_ref.1, f32[16,8,128]{2,1,0:T(8,128)} %m_ref.1, s32[8,128]{1,0:T(8,128)} %pad.4.agg_ref, f32[128,2048]{1,0:T(8,128)} %inverse_ref.1), custom_call_target="tpu_custom_call" | custom-call | tf_op jit(solution)/shard_map/pallas_call | solution.py:427
  172.7 1.5 copy.7

commit v2 on v1

--- a/solution.py
+++ b/solution.py
@@ -27,18 +27,23 @@
         EXCHANGES += [(0, 1)]
 
 
+def neighbours(level):
+    reach = REACH[level]
+    steps = [(x, y, z) for x in (-1, 0, 1) for y in range(-reach, reach + 1) for z in (-1, 0, 1)]
+    return [step for step in steps if step != (0, 0, 0)]
+
+
 def exchange_scratch(level, fields):
     nx = SIZE[level][0]
     planes = PLANES[level]
     reach = REACH[level]
-    copies = 4 + 2 * reach
+    copies = len(neighbours(level))
     return [
         pltpu.VMEM((fields, nx, 8, 128), F32),
         pltpu.VMEM((2, fields, HALO, 8, 128), F32),
-        pltpu.VMEM((fields, planes, 8, 128), F32),
         pltpu.VMEM((2 * reach, fields, planes, 8, 128), F32),
-        pltpu.VMEM((2, fields, ROWS, 128), F32),
-        pltpu.VMEM((2, fields, ROWS, 128), F32),
+        pltpu.VMEM((2, fields, 8, 128), F32),
+        pltpu.VMEM((2, 3, 2 * reach + 1, fields, 8, 128), F32),
         pltpu.SemaphoreType.DMA((copies,)),
         pltpu.SemaphoreType.DMA((copies,)),
     ]
@@ -59,7 +64,7 @@
     ]
 
 
-PER_EXCHANGE = 8
+PER_EXCHANGE = 7
 PER_COARSE = 10
 
 
@@ -67,17 +72,21 @@
     return lax.rem(lax.axis_index(axis) + (step + COUNT[axis]), COUNT[axis])
 
 
-def send(src, dst, send_sem, recv_sem, axis, step):
+def send_to(src, dst, send_sem, recv_sem, steps):
     copy = pltpu.make_async_remote_copy(
         src_ref=src,
         dst_ref=dst,
         send_sem=send_sem,
         recv_sem=recv_sem,
-        device_id={axis: peer(axis, step)},
+        device_id={axis: peer(axis, step) for axis, step in zip(AXES, steps) if step != 0},
         device_id_type=MESH,
     )
     copy.start()
     return copy
+
+
+def send(src, dst, send_sem, recv_sem, axis, step):
+    return send_to(src, dst, send_sem, recv_sem, [step if axis == name else 0 for name in AXES])
 
 
 def iota(shape, dim):
@@ -92,88 +101,87 @@
     return pltpu.roll(value, shift, axis)
 
 
+def slab_of(step):
+    return 2 * (abs(step) - 1) + (0 if step > 0 else 1)
+
+
+def join_rows(level, value, near):
+    row = iota(value.shape, 1)
+    if level == 0:
+        first = value
+        second = jnp.where(row < 4, near(1), near(-1))
+    elif level == 1:
+        first = jnp.where(row < 4, value, turn_by(near(1), 4, 1))
+        second = turn_by(near(-1), 4, 1)
+    else:
+        far = jnp.where(row < 4, turn_by(near(1), 2, 1), turn_by(near(2), 4, 1))
+        first = jnp.where(row < 2, value, far)
+        second = jnp.where(row < 6, turn_by(near(-2), 4, 1), turn_by(near(-1), 6, 1))
+    return jnp.concatenate([first, second], axis=1)
+
+
 def exchange(jobs):
     copies = []
     for level, bufs, fields in jobs:
-        own, from_x, _, _, _, _, ss, rs = bufs
-        nx = SIZE[level][0]
+        own, from_x, from_y, edges, from_z, ss, rs = bufs
+        nx, _, nz = SIZE[level]
+        reach = REACH[level]
+        lane = iota((8, 128), 1)
         for i, value in enumerate(fields):
             own[i] = value
-        copies.append(send(own.at[:, 0:HALO], from_x.at[0], ss.at[0], rs.at[0], "gx", -1))
-        copies.append(send(own.at[:, nx - HALO : nx], from_x.at[1], ss.at[1], rs.at[1], "gx", 1))
-    for copy in copies:
-        copy.wait()
-    copies = []
-    for level, bufs, fields in jobs:
-        own, from_x, slab, from_y, _, _, ss, rs = bufs
-        nx = SIZE[level][0]
-        for i in range(len(fields)):
-            slab[i, 0:nx] = own[i]
-            slab[i, nx : nx + HALO] = from_x[0, i]
-            slab[i, nx + HALO : nx + 2 * HALO] = from_x[1, i]
-        for step in range(1, REACH[level] + 1):
-            for side, way in ((0, -1), (1, 1)):
-                at = 2 * (step - 1) + side
-                copies.append(send(slab, from_y.at[at], ss.at[2 + at], rs.at[2 + at], "gy", way * step))
-    for copy in copies:
-        copy.wait()
-    copies = []
-    columns = []
-    for level, bufs, fields in jobs:
-        _, _, slab, from_y, edges, from_z, ss, rs = bufs
-        planes = PLANES[level]
-        nz = SIZE[level][2]
-        row = iota((planes, 8, 128), 1)
-        lane = iota((ROWS, 128), 1)
-        mine = []
-        for i in range(len(fields)):
-            value = slab[i]
-            if level == 0:
-                first = value
-                second = jnp.where(row < 4, from_y[0, i], from_y[1, i])
-            elif level == 1:
-                first = jnp.where(row < 4, value, turn_by(from_y[0, i], 4, 1))
-                second = turn_by(from_y[1, i], 4, 1)
-            else:
-                far = jnp.where(row < 4, turn_by(from_y[0, i], 2, 1), turn_by(from_y[2, i], 4, 1))
-                first = jnp.where(row < 2, value, far)
-                second = jnp.where(row < 6, turn_by(from_y[3, i], 4, 1), turn_by(from_y[1, i], 6, 1))
-            column = jnp.concatenate([first, second], axis=1)
-            mine.append(column)
-            low = jnp.zeros((ROWS, 128), F32)
-            high = jnp.zeros((ROWS, 128), F32)
-            for p in range(planes):
+            low = jnp.zeros((8, 128), F32)
+            high = jnp.zeros((8, 128), F32)
+            for p in range(nx):
                 here = (lane >= 4 * p) & (lane < 4 * p + 4)
-                low = jnp.where(here, turn_by(column[p], 4 * p, 1), low)
-                high = jnp.where(here, turn_by(column[p], 4 * p - (nz - 4), 1), high)
+                low = jnp.where(here, turn_by(value[p], 4 * p, 1), low)
+                high = jnp.where(here, turn_by(value[p], 4 * p - (nz - 4), 1), high)
             edges[0, i] = low
             edges[1, i] = high
-        columns.append(mine)
-        at = 2 + 2 * REACH[level]
-        copies.append(send(edges.at[0], from_z.at[0], ss.at[at], rs.at[at], "gz", -1))
-        copies.append(send(edges.at[1], from_z.at[1], ss.at[at + 1], rs.at[at + 1], "gz", 1))
+        order = sorted(enumerate(neighbours(level)), key=lambda item: -sum(abs(step) for step in item[1]))
+        for at, (dx, dy, dz) in order:
+            part = pl.ds(0, nx) if dx == 0 else pl.ds(0, HALO) if dx < 0 else pl.ds(nx - HALO, HALO)
+            there = pl.ds(0, nx) if dx == 0 else pl.ds(nx, HALO) if dx < 0 else pl.ds(nx + HALO, HALO)
+            if dz != 0:
+                side = 0 if dz < 0 else 1
+                src, dst = edges.at[side], from_z.at[side, 1 - dx, reach - dy]
+            elif dy != 0:
+                src, dst = own.at[:, part], from_y.at[slab_of(-dy), :, there]
+            else:
+                src, dst = own.at[:, part], from_x.at[0 if dx < 0 else 1]
+            copies.append(send_to(src, dst, ss.at[at], rs.at[at], (dx, dy, dz)))
     for copy in copies:
         copy.wait()
     rings = []
-    for (level, bufs, fields), mine in zip(jobs, columns):
-        from_z = bufs[5]
+    for level, bufs, fields in jobs:
+        own, from_x, from_y, edges, from_z, ss, rs = bufs
+        nx, _, nz = SIZE[level]
+        reach = REACH[level]
         planes = PLANES[level]
-        nz = SIZE[level][2]
         lane = iota((ROWS, 128), 1)
         out = []
         for i in range(len(fields)):
-            right = from_z[0, i]
-            left = from_z[1, i]
+            block = jnp.concatenate([own[i], from_x[0, i], from_x[1, i]], axis=0)
+            column = join_rows(level, block, lambda step: from_y[slab_of(step), i])
+            packed = [
+                [
+                    join_rows(
+                        level,
+                        from_z[side, x, reach, i][None],
+                        lambda step: from_z[side, x, reach + step, i][None],
+                    )[0]
+                    for x in range(3)
+                ]
+                for side in range(2)
+            ]
             made = []
             for p in range(planes):
-                after = turn_by(right, nz - 4 * p, 1)
-                before = turn_by(left, 124 - 4 * p, 1)
+                x, base = (1, p) if p < nx else (2, p - nx) if p < nx + HALO else (0, p - 2 * HALO)
+                after = turn_by(packed[0][x], nz - 4 * base, 1)
+                before = turn_by(packed[1][x], 124 - 4 * base, 1)
                 if level == 0:
-                    side = jnp.where(lane < 64, after, before)
-                    made.append(jnp.concatenate([mine[i][p], side], axis=1))
+                    made.append(jnp.concatenate([column[p], jnp.where(lane < 64, after, before)], axis=1))
                 else:
-                    side = jnp.where(lane < 100, after, before)
-                    made.append(jnp.where(lane < nz, mine[i][p], side))
+                    made.append(jnp.where(lane < nz, column[p], jnp.where(lane < 100, after, before)))
             out.append(jnp.stack(made, axis=0))
         rings.append(out)
     return rings
@@ -266,6 +274,14 @@
     return wide.reshape(PLANES[level], ROWS, LANES[level])
 
 
+def all_peers():
+    steps = neighbours(2)
+    steps += [(0, step, 0) for step in range(1, 16)]
+    steps += [(step, 0, 0) for step in range(1, 4)]
+    steps += [(0, 0, step) for step in range(1, 8)]
+    return {tuple(step % COUNT[axis] for axis, step in zip(AXES, triple)) for triple in steps}
+
+
 def kernel(f_ref, k_ref, m_ref, agg_ref, inverse_ref, out_ref, *scratch):
     n_ex = len(EXCHANGES) * PER_EXCHANGE
     ex_bufs = [scratch[PER_EXCHANGE * e : PER_EXCHANGE * (e + 1)] for e in range(len(EXCHANGES))]
@@ -276,10 +292,11 @@
     source = keep[19:22]
 
     barrier = pltpu.get_barrier_semaphore()
-    for axis in AXES:
-        for step in range(1, COUNT[axis]):
-            pl.semaphore_signal(barrier, inc=1, device_id={axis: peer(axis, step)}, device_id_type=MESH)
-    pl.semaphore_wait(barrier, sum(COUNT[axis] - 1 for axis in AXES))
+    greeted = sorted(all_peers())
+    for steps in greeted:
+        target = {axis: peer(axis, step) for axis, step in zip(AXES, steps) if step != 0}
+        pl.semaphore_signal(barrier, inc=1, device_id=target, device_id_type=MESH)
+    pl.semaphore_wait(barrier, len(greeted))
 
     pools = [pool_matrices(0), pool_matrices(1)]
     ks, ms = [k_ref[...]], [m_ref[...]]

time: 174 us -> 137 us (0.79)
  Pallas kernels: 171 us -> 134 us
    pallas_call x1, Pallas kernels: 171 us -> 134 us  [local(): pl.pallas_call(kernel, out_shape=jax.ShapeDtypeStruct(right_side.shape, F...]
where the time goes in v2:
time: 137 us
  Pallas kernels  134 us (98%)
  local copies, waits for them, and re-layouts  2.76 us (2%)
    pallas_call x1, Pallas kernels, local(): pl.pallas_call(kernel, out_shape=jax.ShapeDtypeStruct(right_side.shape, F...  134 us

profile of v2, /device:TPU:1, one launch (start us, length us, event | category | flops | bytes accessed | tf_op | source)
XLA Modules:
  0.0 136.7 jit_solution(16456892438502692274)
XLA Ops:
  0.0 1.3 pad.4.agg_ref
  1.3 134.0 %shard_map.55 = f32[16,8,128]{2,1,0:T(8,128)} custom-call(f32[16,8,128]{2,1,0:T(8,128)} %f_ref.1, f32[16,8,128]{2,1,0:T(8,128)} %k_ref.1, f32[16,8,128]{2,1,0:T(8,128)} %m_ref.1, s32[8,128]{1,0:T(8,128)} %pad.4.agg_ref, f32[128,2048]{1,0:T(8,128)} %inverse_ref.1), custom_call_target="tpu_custom_call" | custom-call | tf_op jit(solution)/shard_map/pallas_call | solution.py:444
  135.3 1.5 %copy.7 = f32[16,8,128]{2,1,0:T(8,128)} copy(f32[16,8,128]{2,1,0:T(8,128)} %shard_map.55) | data formatting | bytes 131072

commit v3 on v2

--- a/solution.py
+++ b/solution.py
@@ -36,17 +36,29 @@
 def exchange_scratch(level, fields):
     nx = SIZE[level][0]
     planes = PLANES[level]
-    reach = REACH[level]
     copies = len(neighbours(level))
+    sems = [pltpu.SemaphoreType.DMA((copies,)), pltpu.SemaphoreType.DMA((copies,))]
+    edges = [pltpu.VMEM((2, fields, 8, 128), F32), pltpu.VMEM((2, 3, 3, fields, 8, 128), F32)]
+    if level == 2:
+        nothing = pltpu.VMEM((8, 128), F32)
+        return [
+            pltpu.VMEM((fields, 8, 128), F32),
+            pltpu.VMEM((3, 5, 3, fields, 8, 128), F32),
+            nothing,
+            nothing,
+            nothing,
+        ] + sems
+    if level == 1:
+        return [
+            pltpu.VMEM((2, fields, 8, 128), F32),
+            pltpu.VMEM((3, 3, 2, fields, 8, 128), F32),
+            pltpu.VMEM((8, 128), F32),
+        ] + edges + sems
     return [
         pltpu.VMEM((fields, nx, 8, 128), F32),
         pltpu.VMEM((2, fields, HALO, 8, 128), F32),
-        pltpu.VMEM((2 * reach, fields, planes, 8, 128), F32),
-        pltpu.VMEM((2, fields, 8, 128), F32),
-        pltpu.VMEM((2, 3, 2 * reach + 1, fields, 8, 128), F32),
-        pltpu.SemaphoreType.DMA((copies,)),
-        pltpu.SemaphoreType.DMA((copies,)),
-    ]
+        pltpu.VMEM((2, fields, planes, 8, 128), F32),
+    ] + edges + sems
 
 
 def coarse_scratch():
@@ -54,18 +66,16 @@
         pltpu.VMEM((16, 1, 128), F32),
         pltpu.VMEM((16, 1, 128), F32),
         pltpu.VMEM((1, 128), F32),
-        pltpu.VMEM((4, 1, 128), F32),
-        pltpu.VMEM((1, 128), F32),
-        pltpu.VMEM((8, 1, 128), F32),
+        pltpu.VMEM((32, 1, 128), F32),
         pltpu.VMEM((16, 128), F32),
         pltpu.VMEM((16, 16, 128), F32),
-        pltpu.SemaphoreType.DMA((41,)),
-        pltpu.SemaphoreType.DMA((41,)),
+        pltpu.SemaphoreType.DMA((62,)),
+        pltpu.SemaphoreType.DMA((62,)),
     ]
 
 
 PER_EXCHANGE = 7
-PER_COARSE = 10
+PER_COARSE = 8
 
 
 def peer(axis, step):
@@ -120,62 +130,126 @@
     return jnp.concatenate([first, second], axis=1)
 
 
-def exchange(jobs):
+def pack_edges(value, edges, i, nx, nz):
+    lane = iota((8, 128), 1)
+    low = jnp.zeros((8, 128), F32)
+    high = jnp.zeros((8, 128), F32)
+    for p in range(nx):
+        here = (lane >= 4 * p) & (lane < 4 * p + 4)
+        low = jnp.where(here, turn_by(value[p], 4 * p, 1), low)
+        high = jnp.where(here, turn_by(value[p], 4 * p - (nz - 4), 1), high)
+    edges[0, i] = low
+    edges[1, i] = high
+
+
+def pack_block(level, value):
+    lane = iota((8, 128), 1)
+    row = iota((8, 128), 0)
+    tiles = []
+    for base in range(0, SIZE[level][0], 4):
+        if level == 2:
+            tile = value[base]
+            for q in range(1, 4):
+                tile = jnp.where(lane < 32 * q, tile, turn_by(value[base + q], 32 * q, 1))
+        else:
+            upper = jnp.where(lane < 64, value[base], turn_by(value[base + 1], 64, 1))
+            lower = jnp.where(lane < 64, value[base + 2], turn_by(value[base + 3], 64, 1))
+            tile = jnp.where(row < 4, upper, turn_by(lower, 4, 0))
+        tiles.append(tile)
+    return tiles
+
+
+def unpack_tile(tile, q):
+    return turn_by(turn_by(tile, -64 * (q % 2), 1), -4 * (q // 2), 0)
+
+
+def exchange(jobs, meanwhile=None):
     copies = []
     for level, bufs, fields in jobs:
-        own, from_x, from_y, edges, from_z, ss, rs = bufs
+        own, near, from_y, edges, from_z, ss, rs = bufs
         nx, _, nz = SIZE[level]
         reach = REACH[level]
-        lane = iota((8, 128), 1)
         for i, value in enumerate(fields):
-            own[i] = value
-            low = jnp.zeros((8, 128), F32)
-            high = jnp.zeros((8, 128), F32)
-            for p in range(nx):
-                here = (lane >= 4 * p) & (lane < 4 * p + 4)
-                low = jnp.where(here, turn_by(value[p], 4 * p, 1), low)
-                high = jnp.where(here, turn_by(value[p], 4 * p - (nz - 4), 1), high)
-            edges[0, i] = low
-            edges[1, i] = high
+            if level == 0:
+                own[i] = value
+            elif level == 1:
+                for t, tile in enumerate(pack_block(1, value)):
+                    own[t, i] = tile
+            else:
+                own[i] = pack_block(2, value)[0]
+            if level < 2:
+                pack_edges(value, edges, i, nx, nz)
         order = sorted(enumerate(neighbours(level)), key=lambda item: -sum(abs(step) for step in item[1]))
         for at, (dx, dy, dz) in order:
             part = pl.ds(0, nx) if dx == 0 else pl.ds(0, HALO) if dx < 0 else pl.ds(nx - HALO, HALO)
             there = pl.ds(0, nx) if dx == 0 else pl.ds(nx, HALO) if dx < 0 else pl.ds(nx + HALO, HALO)
-            if dz != 0:
+            if level == 2:
+                src, dst = own, near.at[1 - dx, reach - dy, 1 - dz]
+            elif dz != 0:
                 side = 0 if dz < 0 else 1
                 src, dst = edges.at[side], from_z.at[side, 1 - dx, reach - dy]
+            elif level == 1:
+                if dx == 0:
+                    src, dst = own, near.at[1, 1 - dy]
+                else:
+                    src, dst = own.at[0 if dx < 0 else 1], near.at[1 - dx, 1 - dy, 0]
             elif dy != 0:
                 src, dst = own.at[:, part], from_y.at[slab_of(-dy), :, there]
             else:
-                src, dst = own.at[:, part], from_x.at[0 if dx < 0 else 1]
+                src, dst = own.at[:, part], near.at[0 if dx < 0 else 1]
             copies.append(send_to(src, dst, ss.at[at], rs.at[at], (dx, dy, dz)))
+    if meanwhile is not None:
+        meanwhile()
     for copy in copies:
         copy.wait()
     rings = []
     for level, bufs, fields in jobs:
-        own, from_x, from_y, edges, from_z, ss, rs = bufs
+        own, near, from_y, edges, from_z, ss, rs = bufs
         nx, _, nz = SIZE[level]
-        reach = REACH[level]
         planes = PLANES[level]
         lane = iota((ROWS, 128), 1)
         out = []
-        for i in range(len(fields)):
-            block = jnp.concatenate([own[i], from_x[0, i], from_x[1, i]], axis=0)
-            column = join_rows(level, block, lambda step: from_y[slab_of(step), i])
+        for i, value in enumerate(fields):
+            made = []
+            places = [(1, p) if p < nx else (2, p - nx) if p < nx + HALO else (0, p - 2 * HALO) for p in range(planes)]
+            if level == 2:
+
+                def tile_of(x, step, z):
+                    return (own[i] if (x, step, z) == (1, 0, 1) else near[x, 2 + step, z, i])[None]
+
+                tiles = [
+                    [join_rows(2, tile_of(x, 0, z), lambda step: tile_of(x, step, z))[0] for z in range(3)]
+                    for x in range(3)
+                ]
+                for x, q in places:
+                    middle = turn_by(tiles[x][1], -32 * q, 1)
+                    after = turn_by(tiles[x][2], 32 - 32 * q, 1)
+                    before = turn_by(tiles[x][0], 96 - 32 * q, 1)
+                    made.append(jnp.where(lane < 32, middle, jnp.where(lane < 100, after, before)))
+                out.append(jnp.stack(made, axis=0))
+                continue
+            if level == 1:
+
+                def slab(step):
+                    parts_of = [value[p] for p in range(nx)] if step == 0 else [
+                        unpack_tile(near[1, 1 + step, p // 4, i], p % 4) for p in range(nx)
+                    ]
+                    for x in (2, 0):
+                        parts_of += [unpack_tile(near[x, 1 + step, 0, i], q) for q in range(4)]
+                    return jnp.stack(parts_of, axis=0)
+
+                column = join_rows(1, slab(0), slab)
+            else:
+                block = jnp.concatenate([own[i], near[0, i], near[1, i]], axis=0)
+                column = join_rows(0, block, lambda step: from_y[slab_of(step), i])
             packed = [
                 [
-                    join_rows(
-                        level,
-                        from_z[side, x, reach, i][None],
-                        lambda step: from_z[side, x, reach + step, i][None],
-                    )[0]
+                    join_rows(level, from_z[side, x, 1, i][None], lambda step: from_z[side, x, 1 + step, i][None])[0]
                     for x in range(3)
                 ]
                 for side in range(2)
             ]
-            made = []
-            for p in range(planes):
-                x, base = (1, p) if p < nx else (2, p - nx) if p < nx + HALO else (0, p - 2 * HALO)
+            for p, (x, base) in enumerate(places):
                 after = turn_by(packed[0][x], nz - 4 * base, 1)
                 before = turn_by(packed[1][x], 124 - 4 * base, 1)
                 if level == 0:
@@ -277,8 +351,7 @@
 def all_peers():
     steps = neighbours(2)
     steps += [(0, step, 0) for step in range(1, 16)]
-    steps += [(step, 0, 0) for step in range(1, 4)]
-    steps += [(0, 0, step) for step in range(1, 8)]
+    steps += [(step // 8, 0, step % 8) for step in range(1, 32)]
     return {tuple(step % COUNT[axis] for axis, step in zip(AXES, triple)) for triple in steps}
 
 
@@ -290,26 +363,39 @@
     coef = keep[0:15]
     onehot_lo, onehot_hi, state0, state1 = keep[15:19]
     source = keep[19:22]
+    spread_rows, spread_lanes = keep[22:24], keep[24:26]
 
     barrier = pltpu.get_barrier_semaphore()
     greeted = sorted(all_peers())
     for steps in greeted:
         target = {axis: peer(axis, step) for axis, step in zip(AXES, steps) if step != 0}
         pl.semaphore_signal(barrier, inc=1, device_id=target, device_id_type=MESH)
-    pl.semaphore_wait(barrier, len(greeted))
 
     pools = [pool_matrices(0), pool_matrices(1)]
     ks, ms = [k_ref[...]], [m_ref[...]]
     for level in range(2):
         ks.append(pool(ks[level], pools[level]) * 0.125)
         ms.append(pool(ms[level], pools[level]))
+    pl.semaphore_wait(barrier, len(greeted))
+
+    def meanwhile():
+        for level in range(2):
+            spread_rows[level][...], spread_lanes[level][...] = spread_matrices(level)
+        lanes_of = iota((128, 128), 0)
+        highs = iota((16, 128), 0)
+        for i in range(8):
+            row = agg_ref[i : i + 1, :]
+            onehot_lo[:, 128 * i : 128 * i + 128] = as_chosen(((row & 127) == lanes_of) & (row >= 0))
+            onehot_hi[:, 128 * i : 128 * i + 128] = jnp.where((row >> 7) == highs, 1.0, 0.0)
+
     used = iter(ex_bufs)
     rings = exchange(
         [
             (0, next(used), [ks[0], ms[0], f_ref[...]]),
             (1, next(used), [ks[1], ms[1]]),
             (2, next(used), [ks[2], ms[2]]),
-        ]
+        ],
+        meanwhile,
     )
     for level in range(3):
         kp_ref, sk_ref, d_ref, g_ref, in_ref = coef[5 * level : 5 * level + 5]
@@ -324,13 +410,6 @@
         in_ref[...] = jnp.where(ok, 1.0, 0.0)
     source[0][...] = rings[0][2]
 
-    lanes_of = iota((128, 128), 0)
-    highs = iota((16, 128), 0)
-    for i in range(8):
-        row = agg_ref[i : i + 1, :]
-        onehot_lo[:, 128 * i : 128 * i + 128] = as_chosen(((row & 127) == lanes_of) & (row >= 0))
-        onehot_hi[:, 128 * i : 128 * i + 128] = jnp.where((row >> 7) == highs, 1.0, 0.0)
-
     def residual(level, value):
         kp_ref, sk_ref, d_ref, _, _ = coef[5 * level : 5 * level + 5]
         around = smooth_sum(kp_ref[...] * value)
@@ -346,7 +425,7 @@
         return exchange([(level, next(used), [block])])[0][0]
 
     def aggregate_fix(rest, bufs):
-        mine, from_gy, at_gy, from_gx, at_gx, from_gz, partial, pieces, ss, rs = bufs
+        mine, from_gy, at_gy, from_xz, partial, pieces, ss, rs = bufs
         rows = [rest[i // 2, i % 2 : i % 2 + 1, :] for i in range(8)]
         left = jnp.concatenate([onehot_hi[:, 128 * i : 128 * i + 128] * rows[i] for i in range(8)], axis=1)
         sums = sum(
@@ -365,27 +444,20 @@
             total = total + from_gy[step]
         at_gy[...] = total
         copies = []
-        for step in range(1, 4):
-            copies.append(send(at_gy, from_gx.at[step], ss.at[15 + step], rs.at[15 + step], "gx", step))
+        for step in range(1, 32):
+            steps = (step // 8, 0, step % 8)
+            copies.append(send_to(at_gy, from_xz.at[step], ss.at[15 + step], rs.at[15 + step], steps))
         for copy in copies:
             copy.wait()
-        for step in range(1, 4):
-            total = total + from_gx[step]
-        at_gx[...] = total
-        copies = []
-        for step in range(1, 8):
-            copies.append(send(at_gx, from_gz.at[step], ss.at[18 + step], rs.at[18 + step], "gz", step))
-        for copy in copies:
-            copy.wait()
-        for step in range(1, 8):
-            total = total + from_gz[step]
+        for step in range(1, 32):
+            total = total + from_xz[step]
         down = jnp.broadcast_to(total, (128, 128)).T
         for j in range(16):
             product = down * inverse_ref[:, 128 * j : 128 * j + 128]
             partial[j : j + 1, :] = jnp.sum(product, axis=0, keepdims=True)
         copies = []
         for step in range(1, 16):
-            at = 25 + step
+            at = 46 + step
             copies.append(send(partial, pieces.at[step], ss.at[at], rs.at[at], "gy", step))
         for copy in copies:
             copy.wait()
@@ -419,10 +491,10 @@
         fixed = value[0:4, 0:8, :] + aggregate_fix(rest, co_bufs[turn])
         value = swap(2, fixed) * coef[14][...]
         value = sweep(2, sweep(2, value))
-        value = state1[...] + spread(value, spread_matrices(1), 1)
+        value = state1[...] + spread(value, (spread_rows[1][...], spread_lanes[1][...]), 1)
         value = sweep(1, sweep(1, value))
         value = swap(1, value[0:8, 0:8, :]) * coef[9][...]
-        value = state0[...] + spread(value, spread_matrices(0), 0)
+        value = state0[...] + spread(value, (spread_rows[0][...], spread_lanes[0][...]), 0)
         value = sweep(0, sweep(0, value))
         if turn + 1 < CYCLES:
             value = swap(0, value[0:16, 0:8, 0:128]) * coef[4][...]
@@ -441,6 +513,8 @@
         scratch += [ring] * 5
     scratch += [pltpu.VMEM((128, 1024), BF16), pltpu.VMEM((16, 1024), F32), rings[0], rings[1]]
     scratch += rings
+    scratch += [pltpu.VMEM((PLANES[level] * ROWS, PLANES[level + 1] * ROWS), BF16) for level in range(2)]
+    scratch += [pltpu.VMEM((128, LANES[level]), BF16) for level in range(2)]
     return pl.pallas_call(
         kernel,
         out_shape=jax.ShapeDtypeStruct(right_side.shape, F32),

time: 137 us -> 131 us (0.956)
  Pallas kernels: 134 us -> 128 us
    pallas_call x1, Pallas kernels: 134 us -> 128 us  [local(): pl.pallas_call(kernel, out_shape=jax.ShapeDtypeStruct(right_side.shape, F...]
where the time goes in v3:
time: 131 us
  Pallas kernels  128 us (98%)
  local copies, waits for them, and re-layouts  2.76 us (2%)
    pallas_call x1, Pallas kernels, local(): pl.pallas_call(kernel, out_shape=jax.ShapeDtypeStruct(right_side.shape, F...  128 us

profile of v3, /device:TPU:1, one launch (start us, length us, event | category | flops | bytes accessed | tf_op | source)
XLA Modules:
  0.0 131.1 jit_solution(11126563630429603192)
XLA Ops:
  0.0 1.3 pad.4.agg_ref
  1.3 128.4 %shard_map.55 = f32[16,8,128]{2,1,0:T(8,128)} custom-call(f32[16,8,128]{2,1,0:T(8,128)} %f_ref.1, f32[16,8,128]{2,1,0:T(8,128)} %k_ref.1, f32[16,8,128]{2,1,0:T(8,128)} %m_ref.1, s32[8,128]{1,0:T(8,128)} %pad.4.agg_ref, f32[128,2048]{1,0:T(8,128)} %inverse_ref.1), custom_call_target="tpu_custom_call" | custom-call | tf_op jit(solution)/shard_map/pallas_call | solution.py:518
  129.7 1.5 %copy.7 = f32[16,8,128]{2,1,0:T(8,128)} copy(f32[16,8,128]{2,1,0:T(8,128)} %shard_map.55) | data formatting | bytes 131072
